TPU v7x, 512 devices: a whole 4x8x8 slice. The times are simulated.
512 devices in a mesh: dp: 32 (over x, y), expert: 16 (over z, core).
Axes of the slice: x: 4, y: 8, z: 8, core: 2. Of those that a mesh axis runs over, the one named last changes fastest.
Arguments:
- tokens: bfloat16 [8192, 2048], P('expert', 'dp'), may hold values from -6 to 6
- routes: int32 [8192, 2], P('expert'), may hold values from 0 to 15, all different within a row; in each aligned block of 512 rows (0 to 511, 512 to 1023, ...) at most 96 rows name the same one
- scores: int32 [8192, 2], P('expert'), may hold values from 1 to 1023
- gate_weight: bfloat16 [16, 2048, 8192], P('expert', None, 'dp'), may hold values from -0.125 to 0.125
- up_weight: bfloat16 [16, 2048, 8192], P('expert', None, 'dp'), may hold values from -0.125 to 0.125
- down_weight: bfloat16 [16, 8192, 2048], P('expert', 'dp'), may hold values from -0.0625 to 0.0625
Outputs:
- layer_out: bfloat16 [8192, 2048], P('expert', 'dp')
Inputs may be any that keep to these rules, and one draw needn't show every extreme that they name: `routes`: each row names 2 different experts. Within each aligned block of 512 rows no expert is named by more than 96 rows, and in every draw some expert is named by exactly 96 rows of a block.
All inputs are finite; a program needn't handle non-finite values.
Results may differ from a plain program's by a relative error of at most 0.025.
Values may be sent and summed in bfloat16 or wider, within the bound.
A program may use at most 64 MiB of HBM per device.

v0:
```python
import jax
import jax.numpy as jnp
from jax import lax
from jax.sharding import PartitionSpec as P


def shards(tokens, routes, scores, gate_weight, up_weight, down_weight):
    expert_count = lax.axis_size("expert")
    row_count = tokens.shape[0]
    local_cols = tokens.shape[1]
    capacity = 3 * row_count // expert_count
    slot_count = expert_count * capacity
    expert_ids = jnp.arange(expert_count, dtype=jnp.int32)
    onehot = (routes[:, :, None] == expert_ids[None, None, :]).astype(jnp.int32)
    named = jnp.sum(onehot, axis=1)
    earlier = jnp.cumsum(named, axis=0) - named
    slot_rank = jnp.sum(onehot * earlier[:, None, :], axis=2)
    target = routes * capacity + slot_rank
    slot_ids = jnp.arange(slot_count, dtype=jnp.int32)
    placement = jnp.any(target[None, :, :] == slot_ids[:, None, None], axis=2).astype(jnp.bfloat16)
    weight = scores.astype(jnp.float32)
    weight = weight / jnp.sum(weight, axis=1, keepdims=True)
    gate_mat = gate_weight[0]
    up_mat = up_weight[0]
    down_mat = down_weight[0]
    outgoing = jnp.dot(placement, tokens, preferred_element_type=jnp.float32).astype(jnp.bfloat16)
    arrived = lax.all_to_all(
        outgoing.reshape(expert_count, capacity, local_cols),
        "expert",
        split_axis=0,
        concat_axis=0,
        tiled=True,
    )
    arrived = arrived.reshape(slot_count, local_cols)
    piece = lax.all_gather(arrived, "dp", axis=1, tiled=True)
    gate = jnp.dot(piece, gate_mat, preferred_element_type=jnp.float32)
    upval = jnp.dot(piece, up_mat, preferred_element_type=jnp.float32)
    hidden = (jax.nn.silu(gate) * upval).astype(jnp.bfloat16)
    summed = lax.psum_scatter(
        lax.dot_general(
            down_mat, hidden, (((0,), (1,)), ((), ())), preferred_element_type=jnp.float32
        ).astype(jnp.bfloat16),
        "dp",
        scatter_dimension=0,
        tiled=True,
    ).astype(jnp.float32)
    returned = lax.all_to_all(
        summed.reshape(local_cols, expert_count, capacity).astype(jnp.bfloat16),
        "expert",
        split_axis=1,
        concat_axis=1,
        tiled=True,
    ).astype(jnp.float32)
    returned = returned.reshape(local_cols, slot_count)
    first_part = jnp.take(returned, target[:, 0], axis=1)
    second_part = jnp.take(returned, target[:, 1], axis=1)
    combined = (first_part * weight[:, 0][None, :] + second_part * weight[:, 1][None, :]).T
    return combined.astype(jnp.bfloat16)


def solution(mesh):
    return jax.shard_map(
        shards,
        mesh=mesh,
        in_specs=(
            P("expert", "dp"),
            P("expert", None),
            P("expert", None),
            P("expert", None, "dp"),
            P("expert", None, "dp"),
            P("expert", "dp", None),
        ),
        out_specs=P("expert", "dp"),
        check_vma=False,
    )
```

profile of v0, /device:TPU:1, one launch (start us, length us, event | category | flops | bytes accessed | tf_op | source)
XLA Modules:
  0.0 414.6 jit_solution(14097522096676943779)
XLA Ops:
  6.5 0.8 convert_reduce_fusion
  7.3 1.2 reduce-window.6
  8.5 0.2 slice_reduce_fusion
  8.8 0.1 fusion.12
  8.8 0.7 select_reduce_fusion
  9.6 0.7 multiply_add_fusion
  10.3 2.0 fusion.1
  12.2 1.4 convolution_convert_fusion.1
  13.7 0.2 reshape.37
  13.9 0.1 copy.37
  14.0 23.3 %all_to_all.10 = bf16[16,96,64]{1,2,0:T(8,128)(2,1)S(1)} all-to-all(bf16[16,96,64]{1,2,0:T(8,128)(2,1)S(1)} %copy.37), channel_id=1, replica_groups=mesh['dp'=32,'expert'=16] {'expert'}, dimensions={0} | all-to-all | bytes 393216 | tf_op jit(solution)/shard_map/all_to_all | solution.py:27
  37.3 0.2 copy.38
  37.5 0.9 reshape.38
  38.5 0.0 all-gather.2.cloned.1.call-update
  38.5 0.0 copy-start.2
  38.5 0.0 reduce-scatter.4.cloned.1.call-start
  38.5 89.9 %all-gather.2.cloned.1.call-done = bf16[1536,2048]{0,1:T(8,128)(2,1)} async-done(((bf16[1536,64]{0,1:T(8,128)(2,1)}), bf16[1536,2048]{0,1:T(8,128)(2,1)}) %all-gather.2.cloned.1.call-update) | async-done | bytes 6291472 | tf_op jit(solution)/shard_map/all_gather | solution.py:35
  128.4 6.1 %fusion.6 = f32[1536,256]{1,0:T(8,128)} fusion(bf16[1536,2048]{0,1:T(8,128)(2,1)} %all-gather.2.cloned.1.call-done, bf16[1,2048,256]{2,1,0:T(8,128)(2,1)} %param.11), kind=kOutput, calls=%fused_computation.11 | convolution fusion | flops 1610612736 | bytes 8912896 | tf_op jit(solution)/shard_map/dot_general | solution.py:36
  134.5 12.3 %fusion = bf16[2048,1536]{0,1:T(8,128)(2,1)} fusion(bf16[1536,2048]{0,1:T(8,128)(2,1)} %all-gather.2.cloned.1.call-done, f32[1536,256]{1,0:T(8,128)} %fusion.6, bf16[1,256,2048]{2,1,0:T(8,128)(2,1)S(1)} %copy-done, bf16[1,2048,256]{2,1,0:T(8,128)(2,1)S(1)} %copy-done.2), kind=kOutput, calls=%fused_computation.3 | convolution fusion | flops 3226730496 | bytes 16252928 | tf_op jit(solution)/shard_map/dot_general | solution.py:40
  146.8 8.7 %copy.42 = bf16[2048,1536]{1,0:T(8,128)(2,1)} copy(bf16[2048,1536]{0,1:T(8,128)(2,1)} %fusion) | data formatting | bytes 12582912
  155.5 0.0 reduce-scatter.4.cloned.1.call-update
  155.5 0.7 copy-done.1
  156.3 222.8 %reduce-scatter.4.cloned.1.call-done = bf16[64,1536]{1,0:T(8,128)(2,1)} async-done(((bf16[2048,1536]{1,0:T(8,128)(2,1)}), bf16[64,1536]{1,0:T(8,128)(2,1)}) %reduce-scatter.4.cloned.1.call-update) | async-done | bytes 196624
  379.0 1.1 copy.43
  380.2 0.9 copy.39
  381.0 11.6 %all-to-all-start.1 = ((bf16[64,16,96]{2,0,1:T(8,128)(2,1)}), bf16[64,16,96]{2,0,1:T(8,128)(2,1)S(1)}, u32[]{:S(2)}, u32[]{:S(2)}) async-start(bf16[64,16,96]{2,0,1:T(8,128)(2,1)} %copy.39), calls=%async_computation.1 | async-start | bytes 524288 | tf_op jit(solution)/shard_map/all_to_all | solution.py:47
  392.7 11.7 %all-to-all-done.1 = bf16[64,16,96]{2,0,1:T(8,128)(2,1)S(1)} async-done(((bf16[64,16,96]{2,0,1:T(8,128)(2,1)}), bf16[64,16,96]{2,0,1:T(8,128)(2,1)S(1)}, u32[]{:S(2)}, u32[]{:S(2)}) %all-to-all-start.1) | async-done | bytes 196640 | tf_op jit(solution)/shard_map/all_to_all | solution.py:47
  404.4 0.2 copy.40
  404.6 1.0 gather_fusion
  405.6 1.0 gather_fusion.1
  406.6 0.3 fusion.11
  407.0 0.7 copy.41
  (17 shorter events, 0.1 us)
Async XLA Ops:
  6.5 128.0 %copy-start = (bf16[1,256,2048]{2,1,0:T(8,128)(2,1)S(1)}, bf16[1,256,2048]{2,1,0:T(8,128)(2,1)}, u32[]{:S(2)}) copy-start(bf16[1,256,2048]{2,1,0:T(8,128)(2,1)} %param.13) | copy-start | bytes 3145732
  6.5 121.9 %all-gather.2.cloned.1.call-start = ((), (), s32[]{:S(2)}) async-start(), calls=%async_computation.3 | async-start | bytes 6488064 | tf_op jit(solution)/shard_map/all_gather | solution.py:35
  38.5 96.0 %copy-start.2 = (bf16[1,2048,256]{2,1,0:T(8,128)(2,1)S(1)}, bf16[1,2048,256]{2,1,0:T(8,128)(2,1)}, u32[]{:S(2)}) copy-start(bf16[1,2048,256]{2,1,0:T(8,128)(2,1)} %param.12) | copy-start | bytes 3145732
  38.5 340.5 %reduce-scatter.4.cloned.1.call-start = ((), (), s32[]{:S(2)}) async-start(), calls=%async_computation.4 | async-start | bytes 6488064
  155.5 0.7 copy-start.1
  381.0 23.3 %all-to-all-start.1 = ((bf16[64,16,96]{2,0,1:T(8,128)(2,1)}), bf16[64,16,96]{2,0,1:T(8,128)(2,1)S(1)}, u32[]{:S(2)}, u32[]{:S(2)}) async-start(bf16[64,16,96]{2,0,1:T(8,128)(2,1)} %copy.39), calls=%async_computation.1 | async-start | bytes 524288 | tf_op jit(solution)/shard_map/all_to_all | solution.py:47
Sparse Core Ops, SparseCore 0:
  38.6 89.7 all-gather.1
  155.6 223.3 reduce-scatter.3
where the time goes:
time: 415 us
  waiting for transfers between devices  324 us (78%)
  blocking collectives  23.3 us (6%)
  matrix products  19.8 us (5%)
  local copies, waits for them, and re-layouts  16 us (4%)
  between operations  13.5 us (3%)
  starting transfers between devices  11.7 us (3%)
  other arithmetic  5.85 us (1%)
    unnamed x3, waiting for transfers between devices  223 us
    all_gather x1, waiting for transfers between devices, shards(): piece = lax.all_gather(arrived, 'dp', axis=1, tiled=True)  89.9 us
    all_to_all x1, blocking collectives, shards(): lax.all_to_all(outgoing.reshape(expert_count, capacity, local_cols), 'exp...  23.3 us
    dot_general x1, matrix products, shards(): lax.dot_general(down_mat, hidden, (((0,), (1,)), ((), ())), preferred_ele...  12.3 us
    all_to_all x1, waiting for transfers between devices, shards(): lax.all_to_all(summed.reshape(local_cols, expert_count, capacity).astype(...  11.7 us
    all_to_all x1, starting transfers between devices, shards(): lax.all_to_all(summed.reshape(local_cols, expert_count, capacity).astype(...  11.6 us
    unnamed x8, local copies, waits for them, and re-layouts  10.5 us
  transfers between devices with their start and end apart: 3, of which 3 were waited for; matrix products, arithmetic and copies ran while one was open for 0% of the time, Pallas kernels for 0%

commit v1 on v0

--- a/solution.py
+++ b/solution.py
@@ -32,7 +32,9 @@
         tiled=True,
     )
     arrived = arrived.reshape(slot_count, local_cols)
-    piece = lax.all_gather(arrived, "dp", axis=1, tiled=True)
+    piece = jnp.concatenate(
+        lax.all_to_all(jnp.stack([arrived] * lax.axis_size("dp")), "dp", 0, 0), axis=1
+    )
     gate = jnp.dot(piece, gate_mat, preferred_element_type=jnp.float32)
     upval = jnp.dot(piece, up_mat, preferred_element_type=jnp.float32)
     hidden = (jax.nn.silu(gate) * upval).astype(jnp.bfloat16)

time: 415 us -> 471 us (1.13)
  blocking collectives: 23.3 us -> 173 us
  waiting for transfers between devices: 324 us -> 231 us
    all_to_all x0 -> x1, blocking collectives: none -> 150 us  [shards(): lax.all_to_all(jnp.stack([arrived] * lax.axis_size('dp')), 'dp', 0, 0)]
    all_gather x1 -> x0, waiting for transfers between devices: 89.9 us -> none  [shards(): piece = lax.all_gather(arrived, 'dp', axis=1, tiled=True)]
    unnamed x3 -> x2, waiting for transfers between devices: 223 us -> 219 us
    unnamed x8 -> x12, local copies, waits for them, and re-layouts: 10.5 us -> 13.1 us
  transfers between devices with their start and end apart: 3 -> 2, of which waited for: 3 -> 2; matrix products, arithmetic and copies ran while one was open for 0% -> 0% of each run, Pallas kernels for 0% -> 0%
where the time goes in v1:
time: 471 us; the launch traced here: 470 us
  waiting for transfers between devices  231 us (49%)
  blocking collectives  173 us (37%)
  local copies, waits for them, and re-layouts  18.6 us (4%)
  matrix products  16.8 us (4%)
  between operations  13.5 us (3%)
  starting transfers between devices  11.7 us (2%)
  other arithmetic  5.85 us (1%)
    unnamed x2, waiting for transfers between devices  219 us
    all_to_all x1, blocking collectives, shards(): lax.all_to_all(jnp.stack([arrived] * lax.axis_size('dp')), 'dp', 0, 0)  150 us
    all_to_all x1, blocking collectives, shards(): lax.all_to_all(outgoing.reshape(expert_count, capacity, local_cols), 'exp...  23.3 us
    unnamed x12, local copies, waits for them, and re-layouts  13.1 us
    dot_general x1, matrix products, shards(): lax.dot_general(down_mat, hidden, (((0,), (1,)), ((), ())), preferred_ele...  12.3 us
    all_to_all x1, waiting for transfers between devices, shards(): lax.all_to_all(summed.reshape(local_cols, expert_count, capacity).astype(...  11.7 us
    all_to_all x1, starting transfers between devices, shards(): lax.all_to_all(summed.reshape(local_cols, expert_count, capacity).astype(...  11.7 us
  transfers between devices with their start and end apart: 2, of which 2 were waited for; matrix products, arithmetic and copies ran while one was open for 0% of the time, Pallas kernels for 0%

profile of v1, /device:TPU:1, one launch (start us, length us, event | category | flops | bytes accessed | tf_op | source)
XLA Modules:
  0.0 470.3 jit_solution(6540187758719262190)
XLA Ops:
  6.5 0.8 convert_reduce_fusion
  7.3 1.2 reduce-window.6
  8.5 0.2 slice_reduce_fusion
  8.8 0.1 fusion.12
  8.8 0.7 select_reduce_fusion
  9.6 0.7 multiply_add_fusion
  10.3 2.0 fusion.1
  12.2 1.4 convolution_convert_fusion.1
  13.7 0.2 reshape.42
  13.9 0.1 copy.38
  14.0 23.3 %all_to_all.15 = bf16[16,96,64]{1,2,0:T(8,128)(2,1)S(1)} all-to-all(bf16[16,96,64]{1,2,0:T(8,128)(2,1)S(1)} %copy.38), channel_id=1, replica_groups=mesh['dp'=32,'expert'=16] {'expert'}, dimensions={0} | all-to-all | bytes 393216 | tf_op jit(solution)/shard_map/all_to_all | solution.py:27
  37.3 0.2 copy.39
  37.5 0.3 stack_reshape.2
  37.8 0.7 stack.3
  38.5 0.0 copy-start.3
  38.5 149.6 %all_to_all.16 = bf16[32,1536,64]{1,2,0:T(8,128)(2,1)S(1)} all-to-all(bf16[32,1536,64]{1,2,0:T(8,128)(2,1)S(1)} %stack.3), channel_id=1, replica_groups=mesh['dp'=32,'expert'=16] {'dp'}, dimensions={0} | all-to-all | bytes 12582912 | tf_op jit(solution)/shard_map/all_to_all | solution.py:36
  188.1 2.7 copy-done.1
  190.8 3.0 fusion.6
  193.8 12.3 %fusion = bf16[2048,1536]{0,1:T(8,128)(2,1)} fusion(bf16[1536,2048]{0,1:T(8,128)(2,1)} %bitcast.66, f32[1536,256]{1,0:T(8,128)} %fusion.6, bf16[1,256,2048]{2,1,0:T(8,128)(2,1)S(1)} %copy-done, bf16[1,2048,256]{2,1,0:T(8,128)(2,1)S(1)} %copy-done.4), kind=kOutput, calls=%fused_computation.3 | convolution fusion | flops 3226730496 | bytes 16252928 | tf_op jit(solution)/shard_map/dot_general | solution.py:42
  206.1 8.6 %copy.43 = bf16[2048,1536]{1,0:T(8,128)(2,1)} copy(bf16[2048,1536]{0,1:T(8,128)(2,1)} %fusion) | data formatting | bytes 12582912
  214.8 0.0 reduce-scatter.4.cloned.1.call-update
  214.8 0.7 copy-done.2
  215.5 219.2 %reduce-scatter.4.cloned.1.call-done = bf16[64,1536]{1,0:T(8,128)(2,1)} async-done(((bf16[2048,1536]{1,0:T(8,128)(2,1)}), bf16[64,1536]{1,0:T(8,128)(2,1)}) %reduce-scatter.4.cloned.1.call-update) | async-done | bytes 196624
  434.7 1.1 copy.44
  435.9 0.9 copy.40
  436.7 11.7 %all-to-all-start.2 = ((bf16[64,16,96]{2,0,1:T(8,128)(2,1)}), bf16[64,16,96]{2,0,1:T(8,128)(2,1)S(1)}, u32[]{:S(2)}, u32[]{:S(2)}) async-start(bf16[64,16,96]{2,0,1:T(8,128)(2,1)} %copy.40), calls=%async_computation.2 | async-start | bytes 524288 | tf_op jit(solution)/shard_map/all_to_all | solution.py:49
  448.4 11.7 %all-to-all-done.2 = bf16[64,16,96]{2,0,1:T(8,128)(2,1)S(1)} async-done(((bf16[64,16,96]{2,0,1:T(8,128)(2,1)}), bf16[64,16,96]{2,0,1:T(8,128)(2,1)S(1)}, u32[]{:S(2)}, u32[]{:S(2)}) %all-to-all-start.2) | async-done | bytes 196640 | tf_op jit(solution)/shard_map/all_to_all | solution.py:49
  460.1 0.2 copy.41
  460.3 1.0 gather_fusion
  461.3 1.0 gather_fusion.1
  462.4 0.3 fusion.11
  462.7 0.7 copy.42
  (20 shorter events, 0.1 us)
Async XLA Ops:
  6.5 187.3 %copy-start = (bf16[1,256,2048]{2,1,0:T(8,128)(2,1)S(1)}, bf16[1,256,2048]{2,1,0:T(8,128)(2,1)}, u32[]{:S(2)}) copy-start(bf16[1,256,2048]{2,1,0:T(8,128)(2,1)} %param.13) | copy-start | bytes 3145732
  6.5 428.2 %reduce-scatter.4.cloned.1.call-start = ((), (), s32[]{:S(2)}) async-start(), calls=%async_computation.4 | async-start | bytes 6488064
  38.5 152.3 %copy-start.3 = (bf16[1,2048,256]{2,1,0:T(8,128)(2,1)S(1)}, bf16[1,2048,256]{2,1,0:T(8,128)(2,1)}, u32[]{:S(2)}) copy-start(bf16[1,2048,256]{2,1,0:T(8,128)(2,1)} %param.11) | copy-start | bytes 3145732
  188.1 2.7 copy-start.1
  190.8 3.0 copy-start.4
  214.8 0.7 copy-start.2
  436.7 23.4 %all-to-all-start.2 = ((bf16[64,16,96]{2,0,1:T(8,128)(2,1)}), bf16[64,16,96]{2,0,1:T(8,128)(2,1)S(1)}, u32[]{:S(2)}, u32[]{:S(2)}) async-start(bf16[64,16,96]{2,0,1:T(8,128)(2,1)} %copy.40), calls=%async_computation.2 | async-start | bytes 524288 | tf_op jit(solution)/shard_map/all_to_all | solution.py:49
Sparse Core Ops, SparseCore 0:
  214.9 219.7 reduce-scatter.3
